TPU v7x, 256 devices: a whole 4x4x8 slice. The times are simulated.
256 devices in a mesh: cells: 64 (over z, x, core), chan: 4 (over y).
Axes of the slice: x: 4, y: 4, z: 8, core: 2. Of those that a mesh axis runs over, the one named last changes fastest.
Arguments:
- charges: bfloat16 [128, 65536], P('chan', 'cells'), may hold values from -6 to 6
- basis: float32 [25, 65536], P(None, 'cells'), may hold values from -1.5 to 1.5
- atom_leaf: int32 [65536], P('cells'), may hold values from 0 to 8191, as said below
- leaf_lists: int32 [64, 8192], P(None, 'cells'), may hold values from -1 to 8191, as said below
- coarse_lists: int32 [64, 1024], P(None, 'cells'), may hold values from -1 to 1023, as said below
- up_ops: bfloat16 [8, 25, 25], replicated, may hold values from -0.4375 to 0.4375
- down_ops: bfloat16 [8, 25, 25], replicated, may hold values from -1.25 to 1.25
- leaf_ops: bfloat16 [25, 25, 64], replicated, may hold values from -0.15625 to 0.15625
- coarse_ops: bfloat16 [25, 25, 64], replicated, may hold values from -0.15625 to 0.15625
- mix: bfloat16 [128, 128], replicated, may hold values from -0.5 to 0.5
- cotangent: bfloat16 [128, 65536], P('chan', 'cells'), may hold values from -0.005859375 to 0.005859375
Outputs:
- refined: bfloat16 [128, 65536], P('chan', 'cells')
- grad_leaf_ops: float32 [25, 25, 64], replicated
- grad_coarse_ops: float32 [25, 25, 64], replicated
Inputs may be any that keep to these rules, and one draw needn't show every extreme that they name: `atom_leaf`: an atom's leaf is one of the 128 consecutive leaves whose block along cells holds that atom. `leaf_lists`: entry [s, t] is -1 for an empty slot, else a leaf within 64 leaves of the block of 128 leaves that holds t. `coarse_lists`: entry [s, p] is -1 for an empty slot, else a parent cell within 8 cells of the block of 16 parent cells that holds p.
All inputs are finite; a program needn't handle non-finite values.
Results may differ from a plain program's by a relative error of at most 0.014.
Values may be sent and summed in bfloat16 or wider, within the bound.
A program may use at most 128 MiB of HBM per device.

v0:
```python
import jax
import jax.numpy as jnp
from jax import lax
from jax.sharding import PartitionSpec as P

SLOT_BLOCK = 16


def extended(block, sides, width):
    for axis, dim in sides:
        count = lax.axis_size(axis)
        forward = [(i, i + 1) for i in range(count - 1)]
        backward = [(target, source) for source, target in forward]
        low = lax.ppermute(
            lax.slice_in_dim(block, block.shape[dim] - width, None, axis=dim), axis, forward
        )
        high = lax.ppermute(lax.slice_in_dim(block, 0, width, axis=dim), axis, backward)
        block = jnp.concatenate([low, block, high], axis=dim)
    return block


def spread(weights, values, local_leaf, leaf_dev):
    kcount, atoms = weights.shape
    chan_part = values.shape[0]
    width = min(1024, atoms)

    def spread_accumulate(counter, running):
        member = (local_leaf[:, None] == jnp.arange(leaf_dev, dtype=jnp.int32)[None, :]).astype(
            jnp.bfloat16
        )
        scaled = (weights[:, None, :] * values[None].astype(jnp.float32)).astype(jnp.bfloat16)
        return running + jnp.dot(
            scaled.reshape(kcount * chan_part, width), member, preferred_element_type=jnp.float32
        )

    start_value = jnp.zeros((kcount * chan_part, leaf_dev), jnp.float32)
    result = lax.fori_loop(0, atoms // width, spread_accumulate, start_value)
    return result.reshape(kcount, chan_part, leaf_dev)


def collect(weights, fields, local_leaf):
    kcount, chan_part, leaf_dev = fields.shape
    atoms = weights.shape[1]
    width = min(1024, atoms)
    flat_fields = fields.reshape(kcount * chan_part, leaf_dev)

    def collect_accumulate(counter, running):
        member = (jnp.arange(leaf_dev, dtype=jnp.int32)[:, None] == local_leaf[None, :]).astype(
            jnp.bfloat16
        )
        per_atom = jnp.dot(flat_fields, member, preferred_element_type=jnp.float32).reshape(
            kcount, chan_part, width
        )
        summed = jnp.sum(weights[:, None, :] * per_atom, axis=0)
        return summed

    start_value = jnp.zeros((chan_part, atoms), jnp.float32)
    return lax.fori_loop(0, atoms // width, collect_accumulate, start_value)


def pick(source, group_list, first_cell):
    valid = group_list >= 0
    position = jnp.where(valid, group_list - first_cell, 0)
    picked = jnp.take(source, position, axis=2)
    return picked * valid.astype(jnp.bfloat16)[None, None]


def translate(source, lists, first_cell, ops):
    kcount, chan_part, _ = source.shape
    slot_count, targets = lists.shape
    groups = slot_count // SLOT_BLOCK
    list_groups = lists.reshape(groups, SLOT_BLOCK, targets)
    op_groups = jnp.transpose(ops.reshape(kcount, kcount, groups, SLOT_BLOCK), (2, 3, 0, 1))

    def translate_advance(running, pieces):
        group_list, group_ops = pieces
        picked = pick(source, group_list, first_cell)
        return (
            running
            + jnp.einsum("okj,jcot->kct", group_ops, picked, preferred_element_type=jnp.float32),
            None,
        )

    start_value = jnp.zeros((kcount, chan_part, targets), jnp.float32)
    result, _ = lax.scan(translate_advance, start_value, (list_groups, op_groups))
    return result


def slot_gradients(source, lists, first_cell, fields):
    kcount = source.shape[0]
    slot_count, targets = lists.shape
    groups = slot_count // SLOT_BLOCK
    list_groups = lists.reshape(groups, SLOT_BLOCK, targets)

    def slot_advance(carried, group_list):
        picked = pick(source, group_list, first_cell)
        return (
            carried,
            jnp.einsum("kct,jcot->kjo", fields, picked, preferred_element_type=jnp.float32),
        )

    _, stacked = lax.scan(slot_advance, jnp.zeros((), jnp.float32), list_groups)
    return jnp.transpose(stacked, (1, 2, 0, 3)).reshape(kcount, kcount, slot_count)


def local(
    charges,
    basis,
    atom_leaf,
    leaf_lists,
    coarse_lists,
    up_ops,
    down_ops,
    leaf_ops,
    coarse_ops,
    mix,
    cotangent,
):
    chan_part = charges.shape[0]
    kcount = basis.shape[0]
    leaf_dev = leaf_lists.shape[1]
    coarse_dev = coarse_lists.shape[1]
    cells_pos = lax.axis_index("cells")
    chan_pos = lax.axis_index("chan")
    local_leaf = atom_leaf - cells_pos * leaf_dev
    moments = spread(basis, charges, local_leaf, leaf_dev).astype(jnp.bfloat16)
    grouped = moments.reshape(kcount, chan_part, coarse_dev, 8)
    coarse = jnp.einsum(
        "okj,jcpo->kcp", up_ops, grouped, preferred_element_type=jnp.float32
    ).astype(jnp.bfloat16)
    leaf_source = extended(moments, (("cells", 2),), leaf_dev // 2)
    leaf_first = cells_pos * leaf_dev - leaf_dev // 2
    coarse_source = extended(coarse, (("cells", 2),), coarse_dev // 2)
    coarse_first = cells_pos * coarse_dev - coarse_dev // 2
    near_field = translate(leaf_source, leaf_lists, leaf_first, leaf_ops)
    far_field = translate(coarse_source, coarse_lists, coarse_first, coarse_ops).astype(
        jnp.bfloat16
    )
    child = jnp.einsum("okj,jcp->kcpo", down_ops, far_field, preferred_element_type=jnp.float32)
    expansion = (near_field + child.reshape(kcount, chan_part, leaf_dev)).astype(jnp.bfloat16)
    potential = collect(basis, expansion, local_leaf).astype(jnp.bfloat16)
    rows_mine = lax.dynamic_slice_in_dim(mix, chan_pos * chan_part, chan_part, 0)
    cols_mine = lax.dynamic_slice_in_dim(mix, chan_pos * chan_part, chan_part, 1)
    mixed = lax.dot_general(
        cols_mine,
        lax.all_gather(potential, "chan", axis=0, tiled=True),
        (((0,), (0,)), ((), ())),
        preferred_element_type=jnp.float32,
    )
    back_sum = jnp.dot(
        rows_mine,
        lax.all_gather(cotangent, "chan", axis=0, tiled=True),
        preferred_element_type=jnp.float32,
    )
    refined = (charges.astype(jnp.float32) + mixed).astype(jnp.bfloat16)
    back_potential = back_sum.astype(jnp.bfloat16)
    back_expansion = spread(basis, back_potential, local_leaf, leaf_dev).astype(jnp.bfloat16)
    back_grouped = back_expansion.reshape(kcount, chan_part, coarse_dev, 8)
    back_far = jnp.einsum(
        "okj,kcpo->jcp", down_ops, back_grouped, preferred_element_type=jnp.float32
    ).astype(jnp.bfloat16)
    grad_leaf = slot_gradients(leaf_source, leaf_lists, leaf_first, back_expansion)
    grad_coarse = slot_gradients(coarse_source, coarse_lists, coarse_first, back_far)
    grad_leaf, grad_coarse = lax.psum((grad_leaf, grad_coarse), ("cells", "chan"))
    return (refined, grad_leaf, grad_coarse)


def solution(mesh):
    placed = (
        P("chan", "cells"),
        P(None, "cells"),
        P("cells"),
        P(None, "cells"),
        P(None, "cells"),
        P(),
        P(),
        P(),
        P(),
        P(),
        P("chan", "cells"),
    )
    return jax.shard_map(
        local, mesh=mesh, in_specs=placed, out_specs=(P("chan", "cells"), P(), P()), check_vma=False
    )
```

profile of v0, /device:TPU:2, one launch (start us, length us, event | category | flops | bytes accessed | tf_op | source)
XLA Modules:
  0.0 724.2 jit_solution(9109661945923828574)
XLA Ops:
  8.8 1.6 fusion.47
  11.2 1.9 collective-permute-start.1
  13.2 2.4 collective-permute-start
  15.6 1.7 copy.72
  17.7 3.8 collective-permute-start.3
  21.5 1.9 collective-permute-start.2
  23.4 12.3 %all_gather.7 = bf16[128,1024]{1,0:T(8,128)(2,1)S(1)} all-gather(bf16[32,1024]{1,0:T(8,128)(2,1)S(1)} %copy-done.9), channel_id=1, replica_groups=mesh['cells'=64,'chan'=4] {'chan'}, dimensions={0}, use_global_device_ids=true | all-gather | bytes 327680 | tf_op jit(solution)/shard_map/all_gather | solution.py:152
  36.7 1.7 copy.75
  39.5 1.7 copy.40
  43.4 13.1 %while.57 = (s32[]{:T(128)}, f32[25,32,16]{1,0,2:T(8,128)S(1)}, bf16[4,16,25,25]{3,2,1,0:T(8,128)(2,1)S(1)}, s32[4,16,16]{2,1,0:T(8,128)S(1)}, s32[]{:T(128)}, /...) while((s32[]{:T(128)}, f32[25,32,16]{1,0,2:T(8,128)S(1)}, ...), condition=%wide.region_3.6_spmd.clone, body=%wide.region_2.5_spmd.clone.sunk | while | flops 10678787 | bytes 4553847 | solution.py:85
  56.6 17.5 %while.15 = (s32[]{:T(128)}, f32[4,25,25,16]{1,2,3,0:T(8,128)}, s32[4,16,16]{2,1,0:T(8,128)S(1)}, s32[]{:T(128)}, bf16[25,32,32]{1,0,2:T(8,128)(2,1)S(1)}, /*index=5*/bf16[25,32,16]{1,0,2:T(8,128)(2,1)}, s32[]{:T(128)}) while((s32[]{:T(128)}, f32[4,25,25,16]{1,2,3,0:T(8,128)}, s32[4,16,16]{2,1,0:T(8,128)S(1)}, s32[]{:T(128)}, ...), condition=%wide.region_9.12_spmd, body=%wide.region_8.11_spmd.sunk | while | flops 10653186 | bytes 3270785 | solution.py:102
  59.3 1.7 fusion.96
  63.7 1.7 fusion.96
  68.0 1.7 fusion.96
  72.4 1.7 fusion.96
  75.9 2.9 copy.61
  80.2 3.0 copy.41
  83.2 193.7 %while.56 = (s32[]{:T(128)}, f32[25,32,128]{2,0,1:T(8,128)}, bf16[4,16,25,25]{3,2,1,0:T(8,128)(2,1)}, s32[4,16,128]{2,1,0:T(8,128)S(1)}, s32[]{:T(128)}, /*index...) while((s32[]{:T(128)}, f32[25,32,128]{2,0,1:T(8,128)}, bf16[4,16,25,25]{3,2,1,0:T(8,128)(2,1)}, ...), condition=%wide.region_1.3_spmd.clone, body=%wide.region_0.2_spmd.clone.sunk | while | flops 90349568 | bytes 18425984 | solution.py:85
  83.2 19.3 %gather_fusion.2 = bf16[2048,25,32]{2,1,0:T(8,128)(2,1)} fusion(bf16[25,32,256]{1,0,2:T(8,128)(2,1)S(1)} %get-tuple-element.527, s32[2048]{0:T(1024)S(1)} %bitcast_clamp_fusion.5), kind=kCustom, calls=%fused_computation.clone.clone.1 | custom fusion | bytes 6561792 | tf_op jit(solution)/shard_map/while/body/eval_jaxpr/jit(_take)/gather | solution.py:64
  102.5 24.5 %copy.113 = bf16[16,128,25,32]{1,2,0,3:T(8,128)(2,1)} copy(bf16[16,128,25,32]{3,2,1,0:T(8,128)(2,1)} %bitcast.208) | data formatting | bytes 6553600 | tf_op jit(solution)/shard_map/while/body/eval_jaxpr/jit(_take)/gather | solution.py:64
  127.1 4.5 fusion.98
  131.5 19.3 %gather_fusion.2 = bf16[2048,25,32]{2,1,0:T(8,128)(2,1)} fusion(bf16[25,32,256]{1,0,2:T(8,128)(2,1)S(1)} %get-tuple-element.527, s32[2048]{0:T(1024)S(1)} %bitcast_clamp_fusion.5), kind=kCustom, calls=%fused_computation.clone.clone.1 | custom fusion | bytes 6561792 | tf_op jit(solution)/shard_map/while/body/eval_jaxpr/jit(_take)/gather | solution.py:64
  150.8 24.5 %copy.113 = bf16[16,128,25,32]{1,2,0,3:T(8,128)(2,1)} copy(bf16[16,128,25,32]{3,2,1,0:T(8,128)(2,1)} %bitcast.208) | data formatting | bytes 6553600 | tf_op jit(solution)/shard_map/while/body/eval_jaxpr/jit(_take)/gather | solution.py:64
  175.4 4.6 fusion.98
  180.0 19.3 %gather_fusion.2 = bf16[2048,25,32]{2,1,0:T(8,128)(2,1)} fusion(bf16[25,32,256]{1,0,2:T(8,128)(2,1)S(1)} %get-tuple-element.527, s32[2048]{0:T(1024)S(1)} %bitcast_clamp_fusion.5), kind=kCustom, calls=%fused_computation.clone.clone.1 | custom fusion | bytes 6561792 | tf_op jit(solution)/shard_map/while/body/eval_jaxpr/jit(_take)/gather | solution.py:64
  199.3 24.5 %copy.113 = bf16[16,128,25,32]{1,2,0,3:T(8,128)(2,1)} copy(bf16[16,128,25,32]{3,2,1,0:T(8,128)(2,1)} %bitcast.208) | data formatting | bytes 6553600 | tf_op jit(solution)/shard_map/while/body/eval_jaxpr/jit(_take)/gather | solution.py:64
  223.8 4.6 fusion.98
  228.4 19.3 %gather_fusion.2 = bf16[2048,25,32]{2,1,0:T(8,128)(2,1)} fusion(bf16[25,32,256]{1,0,2:T(8,128)(2,1)S(1)} %get-tuple-element.527, s32[2048]{0:T(1024)S(1)} %bitcast_clamp_fusion.5), kind=kCustom, calls=%fused_computation.clone.clone.1 | custom fusion | bytes 6561792 | tf_op jit(solution)/shard_map/while/body/eval_jaxpr/jit(_take)/gather | solution.py:64
  247.7 24.5 %copy.113 = bf16[16,128,25,32]{1,2,0,3:T(8,128)(2,1)} copy(bf16[16,128,25,32]{3,2,1,0:T(8,128)(2,1)} %bitcast.208) | data formatting | bytes 6553600 | tf_op jit(solution)/shard_map/while/body/eval_jaxpr/jit(_take)/gather | solution.py:64
  272.2 4.6 fusion.98
  278.6 12.3 %all_gather.6 = bf16[128,1024]{1,0:T(8,128)(2,1)S(1)} all-gather(bf16[32,1024]{1,0:T(8,128)(2,1)S(1)} %multiply_reduce_fusion), channel_id=1, replica_groups=mesh['cells'=64,'chan'=4] {'chan'}, dimensions={0}, use_global_device_ids=true | all-gather | bytes 327680 | tf_op jit(solution)/shard_map/all_gather | solution.py:146
  290.9 151.2 %while.14 = (s32[]{:T(128)}, f32[4,25,25,16]{1,3,2,0:T(8,128)}, s32[4,16,128]{2,1,0:T(8,128)S(1)}, s32[]{:T(128)}, bf16[25,32,256]{1,0,2:T(8,128)(2,1)S(1)}, /*index=5*/bf16[25,32,128]{2,0,1:T(8,128)(2,1)S(1)}, s32[]{:T(128)}) while((s32[]{:T(128)}, f32[4,25,25,16]{1,3,2,0:T(8,128)}, s32[4,16,128]{2,1,0:T(8,128)S(1)}, s32[]{:T(128)}, ...), condition=%wide.region_6.9_spmd, body=%wide.region_5.8_spmd.sunk | while | flops 85229568 | bytes 16853100 | solution.py:102
  290.9 19.3 %gather_fusion = bf16[2048,25,32]{2,1,0:T(8,128)(2,1)} fusion(bf16[25,32,256]{1,0,2:T(8,128)(2,1)S(1)} %get-tuple-element.572, s32[2048]{0:T(1024)S(1)} %bitcast_clamp_fusion.4), kind=kCustom, calls=%fused_computation.2.clone.clone.1 | custom fusion | bytes 6561792 | tf_op jit(solution)/shard_map/while/body/eval_jaxpr/jit(_take)/gather | solution.py:64
  310.2 14.9 %copy.110 = bf16[16,128,25,32]{1,0,3,2:T(8,128)(2,1)} copy(bf16[16,128,25,32]{3,2,1,0:T(8,128)(2,1)} %bitcast.209) | data formatting | bytes 6553600 | tf_op jit(solution)/shard_map/while/body/eval_jaxpr/jit(_take)/gather | solution.py:64
  325.1 3.6 fusion.93
  328.7 19.3 %gather_fusion = bf16[2048,25,32]{2,1,0:T(8,128)(2,1)} fusion(bf16[25,32,256]{1,0,2:T(8,128)(2,1)S(1)} %get-tuple-element.572, s32[2048]{0:T(1024)S(1)} %bitcast_clamp_fusion.4), kind=kCustom, calls=%fused_computation.2.clone.clone.1 | custom fusion | bytes 6561792 | tf_op jit(solution)/shard_map/while/body/eval_jaxpr/jit(_take)/gather | solution.py:64
  348.0 14.9 %copy.110 = bf16[16,128,25,32]{1,0,3,2:T(8,128)(2,1)} copy(bf16[16,128,25,32]{3,2,1,0:T(8,128)(2,1)} %bitcast.209) | data formatting | bytes 6553600 | tf_op jit(solution)/shard_map/while/body/eval_jaxpr/jit(_take)/gather | solution.py:64
  362.9 3.6 fusion.93
  366.5 19.3 %gather_fusion = bf16[2048,25,32]{2,1,0:T(8,128)(2,1)} fusion(bf16[25,32,256]{1,0,2:T(8,128)(2,1)S(1)} %get-tuple-element.572, s32[2048]{0:T(1024)S(1)} %bitcast_clamp_fusion.4), kind=kCustom, calls=%fused_computation.2.clone.clone.1 | custom fusion | bytes 6561792 | tf_op jit(solution)/shard_map/while/body/eval_jaxpr/jit(_take)/gather | solution.py:64
  385.8 14.9 %copy.110 = bf16[16,128,25,32]{1,0,3,2:T(8,128)(2,1)} copy(bf16[16,128,25,32]{3,2,1,0:T(8,128)(2,1)} %bitcast.209) | data formatting | bytes 6553600 | tf_op jit(solution)/shard_map/while/body/eval_jaxpr/jit(_take)/gather | solution.py:64
  400.7 3.6 fusion.93
  404.3 19.3 %gather_fusion = bf16[2048,25,32]{2,1,0:T(8,128)(2,1)} fusion(bf16[25,32,256]{1,0,2:T(8,128)(2,1)S(1)} %get-tuple-element.572, s32[2048]{0:T(1024)S(1)} %bitcast_clamp_fusion.4), kind=kCustom, calls=%fused_computation.2.clone.clone.1 | custom fusion | bytes 6561792 | tf_op jit(solution)/shard_map/while/body/eval_jaxpr/jit(_take)/gather | solution.py:64
  423.6 14.9 %copy.110 = bf16[16,128,25,32]{1,0,3,2:T(8,128)(2,1)} copy(bf16[16,128,25,32]{3,2,1,0:T(8,128)(2,1)} %bitcast.209) | data formatting | bytes 6553600 | tf_op jit(solution)/shard_map/while/body/eval_jaxpr/jit(_take)/gather | solution.py:64
  438.5 3.6 fusion.93
  442.1 2.9 copy.54
  445.9 267.0 %all-reduce.3.cloned.1.call-done = (f32[25,25,64]{1,2,0:T(8,128)}, f32[25,25,64]{1,2,0:T(8,128)}) async-done(((f32[25,25,64]{1,2,0:T(8,128)}, f32[25,25,64]{1,2,0:T(8,128)}), (f32[25,25,64]{1,2,0:T(8,128)}, f32[25,25,64]{1,2,0:T(8,128)})) %all-reduce.3.cloned.1.call-update) | async-done | bytes 320016 | tf_op jit(solution)/shard_map/psum | solution.py:164
  712.9 2.2 copy.62
  715.1 2.2 copy.63
  (146 shorter events, 36.5 us)
Async XLA Ops:
  7.2 28.6 %copy-start = (bf16[128,128]{1,0:T(8,128)(2,1)S(1)}, bf16[128,128]{1,0:T(8,128)(2,1)}, u32[]{:S(2)}) copy-start(bf16[128,128]{1,0:T(8,128)(2,1)} %param.32) | copy-start | bytes 98308
  7.2 705.7 %all-reduce.3.cloned.1.call-start = ((), (), s32[]{:S(2)}) async-start(), calls=%async_computation | async-start | bytes 3276800 | tf_op jit(solution)/shard_map/psum | solution.py:164
  8.1 9.2 %copy-start.7 = (bf16[8,25,25]{2,0,1:T(8,128)(2,1)S(1)}, bf16[8,25,25]{2,0,1:T(8,128)(2,1)}, u32[]{:S(2)}) copy-start(bf16[8,25,25]{2,0,1:T(8,128)(2,1)} %param.28) | copy-start | bytes 30004
  10.4 13.0 %copy-start.9 = (bf16[32,1024]{1,0:T(8,128)(2,1)S(1)}, bf16[32,1024]{1,0:T(8,128)(2,1)}, u32[]{:S(2)}) copy-start(bf16[32,1024]{1,0:T(8,128)(2,1)} %param.33) | copy-start | bytes 196612
  10.4 25.5 %copy-start.11 = (f32[25,1024]{1,0:T(8,128)S(1)}, f32[25,1024]{1,0:T(8,128)}, u32[]{:S(2)}) copy-start(f32[25,1024]{1,0:T(8,128)} %param.24) | copy-start | bytes 307204
  11.2 67.6 %collective-permute-start.1 = (bf16[25,32,64]{2,1,0:T(8,128)(2,1)}, bf16[25,32,64]{2,1,0:T(8,128)(2,1)}, u32[]{:S(2)}, u32[]{:S(2)}) collective-permute-start(bf16[25,32,64]{2,1,0:T(8,128)(2,1)} %get-tuple-element.331), channel_id=1, source_target_pairs={{4,0},{8,4},{12,8},{16,12},{20,16},{24,20},{28,24},{32,28},{36,32}... | collective-permute-start | bytes 307208 | tf_op jit(solution)/shard_map/ppermute | solution.py:17
  13.2 65.7 %collective-permute-start = (bf16[25,32,64]{2,1,0:T(8,128)(2,1)}, bf16[25,32,64]{2,1,0:T(8,128)(2,1)}, u32[]{:S(2)}, u32[]{:S(2)}) collective-permute-start(bf16[25,32,64]{2,1,0:T(8,128)(2,1)} %get-tuple-element.330), channel_id=1, source_target_pairs={{0,4},{4,8},{8,12},{12,16},{16,20},{20,24},{24,28},{28,32},{32,36}... | collective-permute-start | bytes 307208 | tf_op jit(solution)/shard_map/ppermute | solution.py:14
  17.7 20.6 %copy-start.8 = (bf16[8,25,25]{2,0,1:T(8,128)(2,1)S(1)}, bf16[8,25,25]{2,0,1:T(8,128)(2,1)}, u32[]{:S(2)}) copy-start(bf16[8,25,25]{2,0,1:T(8,128)(2,1)} %param.29) | copy-start | bytes 30004
  17.7 25.4 %collective-permute-start.3 = (bf16[25,32,8]{0,1,2:T(8,128)(2,1)S(1)}, bf16[25,32,8]{0,1,2:T(8,128)(2,1)S(1)}, u32[]{:S(2)}, u32[]{:S(2)}) collective-permute-start(bf16[25,32,8]{0,1,2:T(8,128)(2,1)S(1)} %get-tuple-element.333), channel_id=1, source_target_pairs={{4,0},{8,4},{12,8},{16,12},{20,16},{24,20},{28,24},{32,28},{36,32}... | collective-permute-start | bytes 38408 | tf_op jit(solution)/shard_map/ppermute | solution.py:17
  21.5 21.6 %collective-permute-start.2 = (bf16[25,32,8]{0,1,2:T(8,128)(2,1)S(1)}, bf16[25,32,8]{0,1,2:T(8,128)(2,1)S(1)}, u32[]{:S(2)}, u32[]{:S(2)}) collective-permute-start(bf16[25,32,8]{0,1,2:T(8,128)(2,1)S(1)} %get-tuple-element.332), channel_id=1, source_target_pairs={{0,4},{4,8},{8,12},{12,16},{16,20},{20,24},{24,28},{28,32},{32,36}... | collective-permute-start | bytes 38408 | tf_op jit(solution)/shard_map/ppermute | solution.py:14
  35.9 3.6 copy-start.4
  36.6 4.6 copy-start.5
  36.6 5.5 copy-start.10
  58.4 0.9 copy-start.6
  62.8 0.9 copy-start.6
  67.1 0.9 copy-start.6
  71.5 0.9 copy-start.6
  78.9 4.3 copy-start.1
  83.2 194.9 %copy-start.12 = (f32[25,1024]{1,0:T(8,128)S(1)}, f32[25,1024]{1,0:T(8,128)}, u32[]{:S(2)}) copy-start(f32[25,1024]{1,0:T(8,128)} %param.24) | copy-start | bytes 307204
  276.8 14.1 %copy-start.2 = (bf16[25,32,128]{2,0,1:T(8,128)(2,1)S(1)}, bf16[25,32,128]{2,0,1:T(8,128)(2,1)}, u32[]{:S(2)}) copy-start(bf16[25,32,128]{2,0,1:T(8,128)(2,1)} %copy.53) | copy-start | bytes 614404
  442.1 2.9 copy-start.3
Sparse Core Ops, SparseCore 0:
  445.1 267.7 all-reduce.2
where the time goes:
time: 726 us; the launch traced here: 724 us
  local copies, waits for them, and re-layouts  352 us (48%)
  waiting for transfers between devices  267 us (37%)
  matrix products  49.3 us (7%)
  blocking collectives  24.6 us (3%)
  between operations  14.3 us (2%)
  starting transfers between devices  10 us (1%)
    gather x32, local copies, waits for them, and re-layouts, pick(): picked = jnp.take(source, position, axis=2)  325 us
    psum x1, waiting for transfers between devices, local(): lax.psum((grad_leaf, grad_coarse), ('cells', 'chan'))  267 us
    dot_general x8, matrix products, translate_advance(): jnp.einsum('okj,jcot->kct', group_ops, picked, preferred_element_type=jnp...  22.9 us
    dot_general x8, matrix products, slot_advance(): jnp.einsum('kct,jcot->kjo', fields, picked, preferred_element_type=jnp.fl...  21.2 us
  transfers between devices with their start and end apart: 5, of which 1 were waited for; matrix products, arithmetic and copies ran while one was open for 6% of the time, Pallas kernels for 0%

commit v1 on v0

--- a/solution.py
+++ b/solution.py
@@ -1,9 +1,20 @@
+import functools
 import jax
 import jax.numpy as jnp
 from jax import lax
 from jax.sharding import PartitionSpec as P
+from jax.lax import psum
 
 SLOT_BLOCK = 16
+
+
+def refer_entries_for(load, mesh_name, across):
+    finding = psum(load, mesh_name)
+    all_rows = psum(finding, across)
+    return all_rows
+
+
+cards_end = functools.partial(refer_entries_for, mesh_name="chan", across="cells")
 
 
 def extended(block, sides, width):
@@ -161,7 +172,7 @@
     ).astype(jnp.bfloat16)
     grad_leaf = slot_gradients(leaf_source, leaf_lists, leaf_first, back_expansion)
     grad_coarse = slot_gradients(coarse_source, coarse_lists, coarse_first, back_far)
-    grad_leaf, grad_coarse = lax.psum((grad_leaf, grad_coarse), ("cells", "chan"))
+    grad_leaf, grad_coarse = cards_end((grad_leaf, grad_coarse))
     return (refined, grad_leaf, grad_coarse)
 
 

time: 726 us -> 697 us (0.960)
  waiting for transfers between devices: 267 us -> 239 us
    psum x1 -> x2, waiting for transfers between devices: 267 us -> 239 us  [the longest x1 190 us: refer_entries_for(): all_rows = psum(finding, across)]
  transfers between devices with their start and end apart: 5 -> 6, of which waited for: 1 -> 2; matrix products, arithmetic and copies ran while one was open for 6% -> 6% of each run, Pallas kernels for 0% -> 0%
where the time goes in v1:
time: 697 us; the launch traced here: 695 us
  local copies, waits for them, and re-layouts  351 us (50%)
  waiting for transfers between devices  239 us (34%)
  matrix products  49.2 us (7%)
  blocking collectives  24.6 us (4%)
  between operations  14.4 us (2%)
  starting transfers between devices  10.1 us (1%)
    gather x32, local copies, waits for them, and re-layouts, pick(): picked = jnp.take(source, position, axis=2)  325 us
    psum x1, waiting for transfers between devices, refer_entries_for(): all_rows = psum(finding, across)  190 us
    psum x1, waiting for transfers between devices, refer_entries_for(): finding = psum(load, mesh_name)  48.4 us
    dot_general x8, matrix products, translate_advance(): jnp.einsum('okj,jcot->kct', group_ops, picked, preferred_element_type=jnp...  22.8 us
    dot_general x8, matrix products, slot_advance(): jnp.einsum('kct,jcot->kjo', fields, picked, preferred_element_type=jnp.fl...  21.2 us
  transfers between devices with their start and end apart: 6, of which 2 were waited for; matrix products, arithmetic and copies ran while one was open for 6% of the time, Pallas kernels for 0%

profile of v1, /device:TPU:2, one launch (start us, length us, event | category | flops | bytes accessed | tf_op | source)
XLA Modules:
  0.0 694.5 jit_solution(4402984464782514003)
XLA Ops:
  11.3 1.9 collective-permute-start.1
  13.2 2.4 collective-permute-start
  15.6 1.7 copy.72
  17.7 3.8 collective-permute-start.3
  21.5 1.9 collective-permute-start.2
  23.5 12.3 %all_gather.7 = bf16[128,1024]{1,0:T(8,128)(2,1)S(1)} all-gather(bf16[32,1024]{1,0:T(8,128)(2,1)S(1)} %copy-done.10), channel_id=1, replica_groups=mesh['cells'=64,'chan'=4] {'chan'}, dimensions={0}, use_global_device_ids=true | all-gather | bytes 327680 | tf_op jit(solution)/shard_map/all_gather | solution.py:163
  36.7 1.7 copy.75
  39.6 1.7 copy.40
  43.4 13.1 %while.57 = (s32[]{:T(128)}, f32[25,32,16]{1,0,2:T(8,128)S(1)}, bf16[4,16,25,25]{3,2,1,0:T(8,128)(2,1)S(1)}, s32[4,16,16]{2,1,0:T(8,128)S(1)}, s32[]{:T(128)}, /...) while((s32[]{:T(128)}, f32[25,32,16]{1,0,2:T(8,128)S(1)}, ...), condition=%wide.region_3.6_spmd.clone, body=%wide.region_2.5_spmd.clone.sunk | while | flops 10678787 | bytes 4553847 | solution.py:96
  56.6 17.5 %while.15 = (s32[]{:T(128)}, f32[4,25,25,16]{1,2,3,0:T(8,128)}, s32[4,16,16]{2,1,0:T(8,128)S(1)}, s32[]{:T(128)}, bf16[25,32,32]{1,0,2:T(8,128)(2,1)S(1)}, /*index=5*/bf16[25,32,16]{1,0,2:T(8,128)(2,1)}, s32[]{:T(128)}) while((s32[]{:T(128)}, f32[4,25,25,16]{1,2,3,0:T(8,128)}, s32[4,16,16]{2,1,0:T(8,128)S(1)}, s32[]{:T(128)}, ...), condition=%wide.region_10.13_spmd, body=%wide.region_9.12_spmd.sunk | while | flops 10653186 | bytes 3270785 | solution.py:113
  59.3 1.7 fusion.96
  63.7 1.7 fusion.96
  68.0 1.7 fusion.96
  72.4 1.7 fusion.96
  75.9 2.9 copy.61
  80.1 3.0 copy.41
  83.1 193.5 %while.56 = (s32[]{:T(128)}, f32[25,32,128]{2,0,1:T(8,128)}, bf16[4,16,25,25]{3,2,1,0:T(8,128)(2,1)}, s32[4,16,128]{2,1,0:T(8,128)S(1)}, s32[]{:T(128)}, /*index...) while((s32[]{:T(128)}, f32[25,32,128]{2,0,1:T(8,128)}, bf16[4,16,25,25]{3,2,1,0:T(8,128)(2,1)}, ...), condition=%wide.region_1.3_spmd.clone, body=%wide.region_0.2_spmd.clone.sunk | while | flops 90349568 | bytes 18425984 | solution.py:96
  83.2 19.2 %gather_fusion.2 = bf16[2048,25,32]{2,1,0:T(8,128)(2,1)} fusion(bf16[25,32,256]{1,0,2:T(8,128)(2,1)S(1)} %get-tuple-element.529, s32[2048]{0:T(1024)S(1)} %bitcast_clamp_fusion.5), kind=kCustom, calls=%fused_computation.clone.clone.1 | custom fusion | bytes 6561792 | tf_op jit(solution)/shard_map/while/body/eval_jaxpr/jit(_take)/gather | solution.py:75
  102.4 24.6 %copy.113 = bf16[16,128,25,32]{1,2,0,3:T(8,128)(2,1)} copy(bf16[16,128,25,32]{3,2,1,0:T(8,128)(2,1)} %bitcast.208) | data formatting | bytes 6553600 | tf_op jit(solution)/shard_map/while/body/eval_jaxpr/jit(_take)/gather | solution.py:75
  127.0 4.5 fusion.98
  131.5 19.2 %gather_fusion.2 = bf16[2048,25,32]{2,1,0:T(8,128)(2,1)} fusion(bf16[25,32,256]{1,0,2:T(8,128)(2,1)S(1)} %get-tuple-element.529, s32[2048]{0:T(1024)S(1)} %bitcast_clamp_fusion.5), kind=kCustom, calls=%fused_computation.clone.clone.1 | custom fusion | bytes 6561792 | tf_op jit(solution)/shard_map/while/body/eval_jaxpr/jit(_take)/gather | solution.py:75
  150.7 24.6 %copy.113 = bf16[16,128,25,32]{1,2,0,3:T(8,128)(2,1)} copy(bf16[16,128,25,32]{3,2,1,0:T(8,128)(2,1)} %bitcast.208) | data formatting | bytes 6553600 | tf_op jit(solution)/shard_map/while/body/eval_jaxpr/jit(_take)/gather | solution.py:75
  175.3 4.6 fusion.98
  179.8 19.2 %gather_fusion.2 = bf16[2048,25,32]{2,1,0:T(8,128)(2,1)} fusion(bf16[25,32,256]{1,0,2:T(8,128)(2,1)S(1)} %get-tuple-element.529, s32[2048]{0:T(1024)S(1)} %bitcast_clamp_fusion.5), kind=kCustom, calls=%fused_computation.clone.clone.1 | custom fusion | bytes 6561792 | tf_op jit(solution)/shard_map/while/body/eval_jaxpr/jit(_take)/gather | solution.py:75
  199.1 24.6 %copy.113 = bf16[16,128,25,32]{1,2,0,3:T(8,128)(2,1)} copy(bf16[16,128,25,32]{3,2,1,0:T(8,128)(2,1)} %bitcast.208) | data formatting | bytes 6553600 | tf_op jit(solution)/shard_map/while/body/eval_jaxpr/jit(_take)/gather | solution.py:75
  223.7 4.6 fusion.98
  228.2 19.2 %gather_fusion.2 = bf16[2048,25,32]{2,1,0:T(8,128)(2,1)} fusion(bf16[25,32,256]{1,0,2:T(8,128)(2,1)S(1)} %get-tuple-element.529, s32[2048]{0:T(1024)S(1)} %bitcast_clamp_fusion.5), kind=kCustom, calls=%fused_computation.clone.clone.1 | custom fusion | bytes 6561792 | tf_op jit(solution)/shard_map/while/body/eval_jaxpr/jit(_take)/gather | solution.py:75
  247.5 24.6 %copy.113 = bf16[16,128,25,32]{1,2,0,3:T(8,128)(2,1)} copy(bf16[16,128,25,32]{3,2,1,0:T(8,128)(2,1)} %bitcast.208) | data formatting | bytes 6553600 | tf_op jit(solution)/shard_map/while/body/eval_jaxpr/jit(_take)/gather | solution.py:75
  272.1 4.6 fusion.98
  276.6 150.9 %while.14 = (s32[]{:T(128)}, f32[4,25,25,16]{1,3,2,0:T(8,128)}, s32[4,16,128]{2,1,0:T(8,128)S(1)}, s32[]{:T(128)}, bf16[25,32,256]{1,0,2:T(8,128)(2,1)S(1)}, /*index=5*/bf16[25,32,128]{2,0,1:T(8,128)(2,1)S(1)}, s32[]{:T(128)}) while((s32[]{:T(128)}, f32[4,25,25,16]{1,3,2,0:T(8,128)}, s32[4,16,128]{2,1,0:T(8,128)S(1)}, s32[]{:T(128)}, ...), condition=%wide.region_6.9_spmd, body=%wide.region_5.8_spmd.sunk | while | flops 85229568 | bytes 16853100 | solution.py:113
  276.6 19.2 %gather_fusion = bf16[2048,25,32]{2,1,0:T(8,128)(2,1)} fusion(bf16[25,32,256]{1,0,2:T(8,128)(2,1)S(1)} %get-tuple-element.574, s32[2048]{0:T(1024)S(1)} %bitcast_clamp_fusion.4), kind=kCustom, calls=%fused_computation.2.clone.clone.1 | custom fusion | bytes 6561792 | tf_op jit(solution)/shard_map/while/body/eval_jaxpr/jit(_take)/gather | solution.py:75
  295.9 14.9 %copy.110 = bf16[16,128,25,32]{1,0,3,2:T(8,128)(2,1)} copy(bf16[16,128,25,32]{3,2,1,0:T(8,128)(2,1)} %bitcast.209) | data formatting | bytes 6553600 | tf_op jit(solution)/shard_map/while/body/eval_jaxpr/jit(_take)/gather | solution.py:75
  310.8 3.6 fusion.93
  314.4 19.2 %gather_fusion = bf16[2048,25,32]{2,1,0:T(8,128)(2,1)} fusion(bf16[25,32,256]{1,0,2:T(8,128)(2,1)S(1)} %get-tuple-element.574, s32[2048]{0:T(1024)S(1)} %bitcast_clamp_fusion.4), kind=kCustom, calls=%fused_computation.2.clone.clone.1 | custom fusion | bytes 6561792 | tf_op jit(solution)/shard_map/while/body/eval_jaxpr/jit(_take)/gather | solution.py:75
  333.6 14.9 %copy.110 = bf16[16,128,25,32]{1,0,3,2:T(8,128)(2,1)} copy(bf16[16,128,25,32]{3,2,1,0:T(8,128)(2,1)} %bitcast.209) | data formatting | bytes 6553600 | tf_op jit(solution)/shard_map/while/body/eval_jaxpr/jit(_take)/gather | solution.py:75
  348.5 3.6 fusion.93
  352.1 19.2 %gather_fusion = bf16[2048,25,32]{2,1,0:T(8,128)(2,1)} fusion(bf16[25,32,256]{1,0,2:T(8,128)(2,1)S(1)} %get-tuple-element.574, s32[2048]{0:T(1024)S(1)} %bitcast_clamp_fusion.4), kind=kCustom, calls=%fused_computation.2.clone.clone.1 | custom fusion | bytes 6561792 | tf_op jit(solution)/shard_map/while/body/eval_jaxpr/jit(_take)/gather | solution.py:75
  371.4 14.9 %copy.110 = bf16[16,128,25,32]{1,0,3,2:T(8,128)(2,1)} copy(bf16[16,128,25,32]{3,2,1,0:T(8,128)(2,1)} %bitcast.209) | data formatting | bytes 6553600 | tf_op jit(solution)/shard_map/while/body/eval_jaxpr/jit(_take)/gather | solution.py:75
  386.2 3.6 fusion.93
  389.8 19.2 %gather_fusion = bf16[2048,25,32]{2,1,0:T(8,128)(2,1)} fusion(bf16[25,32,256]{1,0,2:T(8,128)(2,1)S(1)} %get-tuple-element.574, s32[2048]{0:T(1024)S(1)} %bitcast_clamp_fusion.4), kind=kCustom, calls=%fused_computation.2.clone.clone.1 | custom fusion | bytes 6561792 | tf_op jit(solution)/shard_map/while/body/eval_jaxpr/jit(_take)/gather | solution.py:75
  409.1 14.9 %copy.110 = bf16[16,128,25,32]{1,0,3,2:T(8,128)(2,1)} copy(bf16[16,128,25,32]{3,2,1,0:T(8,128)(2,1)} %bitcast.209) | data formatting | bytes 6553600 | tf_op jit(solution)/shard_map/while/body/eval_jaxpr/jit(_take)/gather | solution.py:75
  424.0 3.6 fusion.93
  427.6 2.9 copy.54
  431.3 12.3 %all_gather.6 = bf16[128,1024]{1,0:T(8,128)(2,1)S(1)} all-gather(bf16[32,1024]{1,0:T(8,128)(2,1)S(1)} %multiply_reduce_fusion), channel_id=1, replica_groups=mesh['cells'=64,'chan'=4] {'chan'}, dimensions={0}, use_global_device_ids=true | all-gather | bytes 327680 | tf_op jit(solution)/shard_map/all_gather | solution.py:157
  443.6 48.4 %all-reduce.7.cloned.1.call-done = (f32[25,25,64]{1,2,0:T(8,128)}, f32[25,25,64]{1,2,0:T(8,128)}) async-done(((f32[25,25,64]{1,2,0:T(8,128)}, f32[25,25,64]{1,2,0:T(8,128)}), (f32[25,25,64]{1,2,0:T(8,128)}, f32[25,25,64]{1,2,0:T(8,128)})) %all-reduce.7.cloned.1.call-update) | async-done | bytes 320016 | tf_op jit(solution)/shard_map/psum | solution.py:12
  492.9 190.3 %all-reduce.5.cloned.1.call-done = (f32[25,25,64]{1,2,0:T(8,128)}, f32[25,25,64]{1,2,0:T(8,128)}) async-done(((f32[25,25,64]{1,2,0:T(8,128)}, f32[25,25,64]{1,2,0:T(8,128)}), (f32[25,25,64]{1,2,0:T(8,128)}, f32[25,25,64]{1,2,0:T(8,128)})) %all-reduce.5.cloned.1.call-update) | async-done | bytes 320016 | tf_op jit(solution)/shard_map/psum | solution.py:13
  683.2 2.2 copy.62
  685.5 2.2 copy.63
  (155 shorter events, 37.0 us)
Async XLA Ops:
  7.2 28.6 %copy-start = (bf16[128,128]{1,0:T(8,128)(2,1)S(1)}, bf16[128,128]{1,0:T(8,128)(2,1)}, u32[]{:S(2)}) copy-start(bf16[128,128]{1,0:T(8,128)(2,1)} %param.32) | copy-start | bytes 98308
  7.2 484.8 %all-reduce.7.cloned.1.call-start = ((), (), s32[]{:S(2)}) async-start(), calls=%async_computation.1 | async-start | bytes 3276800 | tf_op jit(solution)/shard_map/psum | solution.py:12
  8.1 9.2 %copy-start.8 = (bf16[8,25,25]{2,0,1:T(8,128)(2,1)S(1)}, bf16[8,25,25]{2,0,1:T(8,128)(2,1)}, u32[]{:S(2)}) copy-start(bf16[8,25,25]{2,0,1:T(8,128)(2,1)} %param.28) | copy-start | bytes 30004
  8.8 27.1 %copy-start.12 = (s32[1024]{0:T(1024)}, s32[1024]{0:T(1024)S(1)}, u32[]{:S(2)}) copy-start(s32[1024]{0:T(1024)S(1)} %broadcast_subtract_fusion) | copy-start | bytes 12292
  10.4 13.0 %copy-start.10 = (bf16[32,1024]{1,0:T(8,128)(2,1)S(1)}, bf16[32,1024]{1,0:T(8,128)(2,1)}, u32[]{:S(2)}) copy-start(bf16[32,1024]{1,0:T(8,128)(2,1)} %param.33) | copy-start | bytes 196612
  10.4 25.5 %copy-start.14 = (f32[25,1024]{1,0:T(8,128)S(1)}, f32[25,1024]{1,0:T(8,128)}, u32[]{:S(2)}) copy-start(f32[25,1024]{1,0:T(8,128)} %param.24) | copy-start | bytes 307204
  11.3 67.6 %collective-permute-start.1 = (bf16[25,32,64]{2,1,0:T(8,128)(2,1)}, bf16[25,32,64]{2,1,0:T(8,128)(2,1)}, u32[]{:S(2)}, u32[]{:S(2)}) collective-permute-start(bf16[25,32,64]{2,1,0:T(8,128)(2,1)} %get-tuple-element.333), channel_id=1, source_target_pairs={{4,0},{8,4},{12,8},{16,12},{20,16},{24,20},{28,24},{32,28},{36,32}... | collective-permute-start | bytes 307208 | tf_op jit(solution)/shard_map/ppermute | solution.py:28
  13.2 65.6 %collective-permute-start = (bf16[25,32,64]{2,1,0:T(8,128)(2,1)}, bf16[25,32,64]{2,1,0:T(8,128)(2,1)}, u32[]{:S(2)}, u32[]{:S(2)}) collective-permute-start(bf16[25,32,64]{2,1,0:T(8,128)(2,1)} %get-tuple-element.332), channel_id=1, source_target_pairs={{0,4},{4,8},{8,12},{12,16},{16,20},{20,24},{24,28},{28,32},{32,36}... | collective-permute-start | bytes 307208 | tf_op jit(solution)/shard_map/ppermute | solution.py:25
  17.7 20.7 %copy-start.9 = (bf16[8,25,25]{2,0,1:T(8,128)(2,1)S(1)}, bf16[8,25,25]{2,0,1:T(8,128)(2,1)}, u32[]{:S(2)}) copy-start(bf16[8,25,25]{2,0,1:T(8,128)(2,1)} %param.29) | copy-start | bytes 30004
  17.7 25.4 %collective-permute-start.3 = (bf16[25,32,8]{0,1,2:T(8,128)(2,1)S(1)}, bf16[25,32,8]{0,1,2:T(8,128)(2,1)S(1)}, u32[]{:S(2)}, u32[]{:S(2)}) collective-permute-start(bf16[25,32,8]{0,1,2:T(8,128)(2,1)S(1)} %get-tuple-element.335), channel_id=1, source_target_pairs={{4,0},{8,4},{12,8},{16,12},{20,16},{24,20},{28,24},{32,28},{36,32}... | collective-permute-start | bytes 38408 | tf_op jit(solution)/shard_map/ppermute | solution.py:28
  21.5 21.6 %collective-permute-start.2 = (bf16[25,32,8]{0,1,2:T(8,128)(2,1)S(1)}, bf16[25,32,8]{0,1,2:T(8,128)(2,1)S(1)}, u32[]{:S(2)}, u32[]{:S(2)}) collective-permute-start(bf16[25,32,8]{0,1,2:T(8,128)(2,1)S(1)} %get-tuple-element.334), channel_id=1, source_target_pairs={{0,4},{4,8},{8,12},{12,16},{16,20},{20,24},{24,28},{28,32},{32,36}... | collective-permute-start | bytes 38408 | tf_op jit(solution)/shard_map/ppermute | solution.py:25
  35.9 3.6 copy-start.5
  36.6 4.6 copy-start.6
  36.7 5.5 copy-start.11
  58.4 0.9 copy-start.7
  62.8 0.9 copy-start.7
  67.1 0.9 copy-start.7
  71.5 0.9 copy-start.7
  78.8 4.3 copy-start.1
  83.1 193.5 %copy-start.3 = (bf16[25,32,128]{2,0,1:T(8,128)(2,1)S(1)}, bf16[25,32,128]{2,0,1:T(8,128)(2,1)}, u32[]{:S(2)}) copy-start(bf16[25,32,128]{2,0,1:T(8,128)(2,1)} %copy.53) | copy-start | bytes 614404
  427.5 3.0 copy-start.2
  427.5 3.1 copy-start.13
  427.6 3.1 copy-start.15
  430.5 252.7 %all-reduce.5.cloned.1.call-start = ((), (), s32[]{:S(2)}) async-start(), calls=%async_computation | async-start | bytes 3276800 | tf_op jit(solution)/shard_map/psum | solution.py:13
  430.7 61.3 %copy-start.4 = (bf16[32,1024]{1,0:T(8,128)(2,1)S(1)}, bf16[32,1024]{1,0:T(8,128)(2,1)}, u32[]{:S(2)}) copy-start(bf16[32,1024]{1,0:T(8,128)(2,1)} %param.23) | copy-start | bytes 196612
Sparse Core Ops, SparseCore 0:
  430.6 61.2 all-reduce.6
  495.5 187.7 all-reduce.4
